TPU v7x, 128 devices: a whole 4x4x4 slice. The times are simulated.
128 devices in a mesh: tm: 16 (over z_lo, y, core), head: 8 (over z_hi, x).
Axes of the slice: x: 4, y: 4, z: 4 (z_hi: 2, z_lo: 2; z = z_hi * 2 + z_lo), core: 2. Of those that a mesh axis runs over, the one named last changes fastest.
Arguments:
- query_vectors: bfloat16 [16384, 4096], P('tm', 'head'), may hold values from -6 to 6
- key_vectors: bfloat16 [16384, 4096], P('tm', 'head'), may hold values from -0.125 to 0.125
- value_vectors: bfloat16 [16384, 4096], P('tm', 'head'), may hold values from -6 to 6
- grad_out: bfloat16 [16384, 4096], P('tm', 'head'), may hold values from -8 to 8
- out_weight: bfloat16 [4096, 4096], P('tm', 'head'), may hold values from -0.09375 to 0.09375
- periods: int32 [32], P('head'), may hold values from 1 to 128, as said below
- log_decay: float32 [32, 16384], P('head', 'tm'), may hold values from -0.1109375 to 0, as said below
Outputs:
- query_gradient: bfloat16 [16384, 4096], P('tm', 'head')
- key_gradient: bfloat16 [16384, 4096], P('tm', 'head')
- value_gradient: bfloat16 [16384, 4096], P('tm', 'head')
- grad_weight: float32 [4096, 4096], P('tm', 'head')
Inputs may be any that keep to these rules, and one draw needn't show every extreme that they name: `periods`: some head has period 1 and some head period 128. `log_decay`: Negative.
All inputs are finite; a program needn't handle non-finite values.
Results may differ from a plain program's by a relative error of at most 0.023.
Values may be sent and summed in bfloat16 or wider, within the bound.
A program may use at most 128 MiB of HBM per device.

v0:
```python
import jax
import jax.numpy as jnp
from jax import lax
from jax.sharding import PartitionSpec as P

DK = 128
BLK = 512


def prefix(value, axis, combine, identity, reverse):
    count, place = (lax.axis_size(axis), lax.axis_index(axis))
    everything = jax.tree.map(
        lambda part, kind: lax.all_gather(part.astype(kind), axis),
        value,
        (jnp.bfloat16, jnp.bfloat16),
    )
    start = jax.tree.map(
        lambda part, zero: jnp.broadcast_to(jnp.asarray(zero, part.dtype), part.shape),
        value,
        identity,
    )

    def turn(k, before):
        at = count - 1 - k if reverse else k
        reached = at > place if reverse else at < place
        new = combine(
            before, jax.tree.map(lambda part, own: part[at].astype(own.dtype), everything, value)
        )
        return jax.tree.map(lambda a, b: jnp.where(reached, a, b), new, before)

    return lax.fori_loop(0, count, turn, start)


def block_mask(cumul, update):
    span_len = cumul.shape[1]
    causal = jnp.arange(span_len)[:, None] >= jnp.arange(span_len)[None, :]
    spread = jnp.where(causal[None], cumul[:, :, None] - cumul[:, None, :], -jnp.inf)
    return jnp.exp(spread) * update[:, None, :]


def pair_weights(query_matrix, key_matrix, value_matrix, gradient_rows, cumul, update_rows):
    decay_mask = block_mask(cumul, update_rows)
    scores = jnp.einsum(
        "thk,shk->hts", query_matrix, key_matrix, preferred_element_type=jnp.float32
    )
    reversed_blocks = jnp.einsum(
        "thv,shv->hts", gradient_rows, value_matrix, preferred_element_type=jnp.float32
    )
    return (
        (scores * decay_mask).astype(jnp.bfloat16),
        (reversed_blocks * decay_mask).astype(jnp.bfloat16),
    )


def layer_output(query_matrix, value_matrix, projection_weight, cumul, state_start):
    within = jnp.einsum(
        "hts,shv->thv", projection_weight, value_matrix, preferred_element_type=jnp.float32
    )
    carried_state = jnp.einsum(
        "qml,mla->qma",
        query_matrix,
        state_start.astype(jnp.bfloat16),
        preferred_element_type=jnp.float32,
    )
    return (within + jnp.exp(cumul).T[:, :, None] * carried_state).astype(jnp.bfloat16)


def input_grads(
    query_matrix,
    key_matrix,
    value_matrix,
    gradient_rows,
    projection_weight,
    reversed_blocks,
    cumul,
    update_rows,
    state_start,
    finish,
):
    state_reduced = state_start.astype(jnp.bfloat16)
    carry_reduced = finish.astype(jnp.bfloat16)
    incoming_gradient = jnp.exp(cumul).T[:, :, None]
    outgoing_gradient = (update_rows * jnp.exp(cumul[:, -1][:, None] - cumul)).T[:, :, None]
    query_gradient = jnp.einsum(
        "gea,agq->egq", reversed_blocks, key_matrix, preferred_element_type=jnp.float32
    ) + incoming_gradient * jnp.einsum(
        "sba,bda->sbd", gradient_rows, state_reduced, preferred_element_type=jnp.float32
    )
    key_gradient = jnp.einsum(
        "rwy,wre->yre", reversed_blocks, query_matrix, preferred_element_type=jnp.float32
    ) + outgoing_gradient * jnp.einsum(
        "wqx,qgx->wqg", value_matrix, carry_reduced, preferred_element_type=jnp.float32
    )
    value_gradient = jnp.einsum(
        "kyp,ykb->pkb", projection_weight, gradient_rows, preferred_element_type=jnp.float32
    ) + outgoing_gradient * jnp.einsum(
        "imx,mxd->imd", key_matrix, carry_reduced, preferred_element_type=jnp.float32
    )
    return (
        query_gradient.astype(jnp.bfloat16),
        key_gradient.astype(jnp.bfloat16),
        value_gradient.astype(jnp.bfloat16),
    )


def combine_carry(earlier, later):
    return (earlier[0] * later[0], later[0][:, None, None] * earlier[1] + later[1])


def per_device(query_vectors, key_vectors, value_vectors, grad_out, out_weight, periods, log_decay):
    tok_rows = query_vectors.shape[0]
    head_count = periods.shape[0]
    block_count = tok_rows // BLK
    full_grad = lax.all_gather(grad_out, "head", axis=1, tiled=True)
    columns = full_grad
    grad_mixed = jnp.dot(
        columns,
        lax.all_gather(out_weight, "tm", axis=0, tiled=True),
        preferred_element_type=jnp.float32,
    ).astype(jnp.bfloat16)
    offset = lax.axis_index("tm") * tok_rows
    positions = offset + jnp.arange(tok_rows, dtype=jnp.int32)
    update = (positions[None, :] % periods[:, None] == 0).astype(jnp.float32)
    step_log = update * periods[:, None].astype(jnp.float32) * log_decay
    cumulative = jnp.cumsum(step_log.reshape(head_count, block_count, BLK), axis=2).transpose(
        1, 0, 2
    )
    updates = update.reshape(head_count, block_count, BLK).transpose(1, 0, 2)

    def blocked(tensor):
        return tensor.reshape(block_count, BLK, head_count, DK)

    query_blocks = blocked(query_vectors)
    key_blocks = blocked(key_vectors)
    value_blocks = blocked(value_vectors)
    grad_blocks = blocked(grad_mixed)
    zero_state = jnp.zeros((head_count, DK, DK), jnp.float32)

    def forward(running, section):
        key_matrix, value_matrix, cumul, update_rows = section
        block_total = cumul[:, -1]
        factor = update_rows * jnp.exp(block_total[:, None] - cumul)
        decay_scaled = (key_matrix.astype(jnp.float32) * factor.T[:, :, None]).astype(jnp.bfloat16)
        outer_product = jnp.einsum(
            "ptz,ptb->tzb", decay_scaled, value_matrix, preferred_element_type=jnp.float32
        )
        return (jnp.exp(block_total)[:, None, None] * running + outer_product, running)

    state_local, state_starts = lax.scan(
        forward, zero_state, (key_blocks, value_blocks, cumulative, updates)
    )

    def backward(carried_in, section):
        query_matrix, gradient_rows, cumul = section
        decay_scaled = (query_matrix.astype(jnp.float32) * jnp.exp(cumul).T[:, :, None]).astype(
            jnp.bfloat16
        )
        outer_product = jnp.einsum(
            "yop,yoj->opj", decay_scaled, gradient_rows, preferred_element_type=jnp.float32
        )
        return (jnp.exp(cumul[:, -1])[:, None, None] * carried_in + outer_product, carried_in)

    grad_local, grad_ends = lax.scan(
        backward, zero_state, (query_blocks, grad_blocks, cumulative), reverse=True
    )
    totals = cumulative[:, :, -1]
    shrink = jnp.exp(jnp.sum(totals, axis=0))
    identity = (jnp.ones((head_count,), jnp.float32), zero_state)
    _, state_in = prefix((shrink, state_local), "tm", combine_carry, identity, False)
    _, grad_in = prefix((shrink, grad_local), "tm", combine_carry, identity, True)
    running_sum = jnp.cumsum(totals, axis=0)
    before = running_sum - totals
    later_sum = jnp.sum(totals, axis=0)[None] - running_sum
    starts = jnp.exp(before)[:, :, None, None] * state_in[None] + state_starts
    finishes = jnp.exp(later_sum)[:, :, None, None] * grad_in[None] + grad_ends
    sections = (
        query_blocks,
        key_blocks,
        value_blocks,
        grad_blocks,
        cumulative,
        updates,
        starts,
        finishes,
    )

    def forward_output(section):
        query_matrix, key_matrix, value_matrix, gradient_rows, cumul, update_rows, state_start = (
            section
        )
        projection_weight, reversed_blocks = pair_weights(
            query_matrix, key_matrix, value_matrix, gradient_rows, cumul, update_rows
        )
        return (
            layer_output(query_matrix, value_matrix, projection_weight, cumul, state_start),
            projection_weight,
            reversed_blocks,
        )

    mixed, weight_blocks, backed_blocks = lax.map(forward_output, sections[:7])
    mixed_rows = mixed.reshape(tok_rows, head_count * DK)
    columns = full_grad
    grad_weight = lax.psum_scatter(
        lax.dot_general(
            columns, mixed_rows, (((0,), (0,)), ((), ())), preferred_element_type=jnp.float32
        ).astype(jnp.bfloat16),
        "tm",
        scatter_dimension=0,
        tiled=True,
    ).astype(jnp.float32)

    def gradient_output(section):
        (
            query_matrix,
            key_matrix,
            value_matrix,
            gradient_rows,
            cumul,
            update_rows,
            state_start,
            finish,
            projection_weight,
            reversed_blocks,
        ) = section
        return input_grads(
            query_matrix,
            key_matrix,
            value_matrix,
            gradient_rows,
            projection_weight,
            reversed_blocks,
            cumul,
            update_rows,
            state_start,
            finish,
        )

    query_gradient, key_gradient, value_gradient = lax.map(
        gradient_output, sections + (weight_blocks, backed_blocks)
    )
    return (
        query_gradient.reshape(tok_rows, head_count * DK),
        key_gradient.reshape(tok_rows, head_count * DK),
        value_gradient.reshape(tok_rows, head_count * DK),
        grad_weight,
    )


def solution(mesh):
    return jax.shard_map(
        per_device,
        mesh=mesh,
        in_specs=(
            P("tm", "head"),
            P("tm", "head"),
            P("tm", "head"),
            P("tm", "head"),
            P("tm", "head"),
            P("head"),
            P("head", "tm"),
        ),
        out_specs=(P("tm", "head"), P("tm", "head"), P("tm", "head"), P("tm", "head")),
        check_vma=False,
    )
```

profile of v0, /device:TPU:6, one launch (start us, length us, event | category | flops | bytes accessed | tf_op | source)
XLA Modules:
  0.0 386.0 jit_solution(7410916782412862764)
XLA Ops:
  11.3 2.4 reduce-window.6
  17.2 2.1 reshape.183
  19.4 1.6 copy.82
  21.0 5.9 %fusion.90 = f32[2,4,512]{1,2,0:T(8,128)} fusion(s32[4]{0:T(128)S(1)} %get-tuple-element.848, s32[2,512]{1,0:T(2,128)S(1)} %add_add_fusion, pred[4]{0:T(512)(128)(4,1)S(1)} %broadcast_compare_fusion), kind=kLoop, calls=%fused_computation.136 | loop fusion | flops 36864 | bytes 20500 | tf_op jit(solution)/shard_map/convert_element_type | solution.py:123
  27.8 4.4 %while.90 = (s32[]{:T(128)}, f32[4,128,128]{2,1,0:T(8,128)S(1)}, f32[2,4,128,128]{3,2,1,0:T(8,128)}, f32[2,4,512]{1,2,0:T(8,128)S(1)}, bf16[2,512,4,128]{1,3,2,0...) while((s32[]{:T(128)}, f32[4,128,128]{2,1,0:T(8,128)S(1)}, ...), condition=%wide.region_5.6_spmd.clone, body=%wide.region_4.5_spmd.clone.sunk | while | flops 68161536 | bytes 2164928 | solution.py:149
  33.9 1.9 copy.77
  37.2 31.3 %all-reduce = bf16[64]{0:T(256)(128)(2,1)S(1)} all-reduce(bf16[64]{0:T(256)(128)(2,1)S(1)} %dynamic-update-slice), channel_id=2, replica_groups=mesh['tm'=16,'head'=8] {'tm'}, use_global_device_ids=true, to_apply=%add | all-reduce | flops 64 | bytes 256
  68.6 2.2 reshape.185
  70.8 2.5 copy.84
  73.4 97.4 %all-gather.8.cloned.1.call-done = bf16[1024,4096]{1,0:T(8,128)(2,1)} async-done(((bf16[1024,512]{1,0:T(8,128)(2,1)}), bf16[1024,4096]{1,0:T(8,128)(2,1)}) %all-gather.8.cloned.1.call-update) | async-done | bytes 8388624 | tf_op jit(solution)/shard_map/all_gather | solution.py:114
  170.8 10.0 %convolution_convert_fusion.1 = bf16[1024,512]{1,0:T(8,128)(2,1)} fusion(bf16[1024,4096]{1,0:T(8,128)(2,1)} %all-gather.8.cloned.1.call-done, bf16[4096,512]{1,0:T(8,128)(2,1)} %all-gather.10.cloned.1.call-done), kind=kOutput, calls=%fused_computation.123 | convolution fusion | flops 4295491584 | bytes 13631488 | tf_op jit(solution)/shard_map/dot_general | solution.py:116
  180.8 2.2 reshape.188
  182.9 1.4 copy.79
  185.1 7.2 %while.92 = (s32[]{:T(128)}, f32[4,128,128]{2,1,0:T(8,128)S(1)}, f32[2,4,128,128]{3,2,1,0:T(8,128)}, f32[2,4,512]{1,2,0:T(8,128)S(1)}, bf16[2,512,4,128]{1,3,2,0...) while((s32[]{:T(128)}, f32[4,128,128]{2,1,0:T(8,128)S(1)}, ...), condition=%wide.region_9.10_spmd.clone, body=%wide.region_8.9_spmd.clone.sunk | while | flops 68157440 | bytes 2148499 | solution.py:163
  193.2 11.9 %all-gather.12.cloned.1.call-done = bf16[64,128,128]{2,1,0:T(8,128)(2,1)} async-done(((bf16[4,128,128]{2,1,0:T(8,128)(2,1)}), bf16[64,128,128]{2,1,0:T(8,128)(2,1)}) %all-gather.12.cloned.1.call-update) | async-done | bytes 2097168 | tf_op jit(solution)/shard_map/all_gather | solution.py:13
  205.1 28.6 %while.91 = (s32[]{:T(128)}, f32[4,128,128]{2,1,0:T(8,128)}, s32[]{:T(128)}, bf16[16,4]{1,0:T(8,128)(2,1)S(1)}, bf16[16,4,128,128]{3,2,1,0:T(8,128)(2,1)}, /*index=5*/s32[]{:T(128)}, s32[]{:T(128)}) while((s32[]{:T(128)}, f32[4,128,128]{2,1,0:T(8,128)}, s32[]{:T(128)}, bf16[16,4]{1,0:T(8,128)(2,1)S(1)}, ...), condition=%wide.region_7.8_spmd.clone, body=%wide.region_6.7_spmd.clone.sunk | while | flops 327688 | bytes 655505 | solution.py:31
  205.1 1.7 fusion.164
  206.8 1.8 fusion.164
  208.6 1.8 fusion.164
  210.4 1.8 fusion.164
  212.2 1.8 fusion.164
  214.0 1.8 fusion.164
  215.8 1.8 fusion.164
  217.6 1.8 fusion.164
  219.4 1.8 fusion.164
  221.2 1.8 fusion.164
  223.0 1.8 fusion.164
  224.8 1.8 fusion.164
  226.6 1.8 fusion.164
  228.4 1.8 fusion.164
  230.2 1.8 fusion.164
  232.0 1.8 fusion.164
  233.7 7.0 %all-gather.14.cloned.1.call-done = bf16[64,128,128]{2,1,0:T(8,128)(2,1)} async-done(((bf16[4,128,128]{2,1,0:T(8,128)(2,1)}), bf16[64,128,128]{2,1,0:T(8,128)(2,1)}) %all-gather.14.cloned.1.call-update) | async-done | bytes 2097168 | tf_op jit(solution)/shard_map/all_gather | solution.py:13
  240.7 17.0 %while.93 = (s32[]{:T(128)}, f32[4,128,128]{2,1,0:T(8,128)S(1)}, s32[]{:T(128)}, bf16[16,4]{1,0:T(8,128)(2,1)S(1)}, bf16[16,4,128,128]{3,2,1,0:T(8,128)(2,1)}, /*index=5*/s32[]{:T(128)}, s32[]{:T(128)}, s32[]{:T(128)}, s32[]{:T(128)}) while((s32[]{:T(128)}, f32[4,128,128]{2,1,0:T(8,128)S(1)}, s32[]{:T(128)}, ...), condition=%wide.region_11.12_spmd.clone, body=%wide.region_10.11_spmd.clone.sunk | while | flops 327692 | bytes 655567 | solution.py:31
  257.8 2.1 multiply_add_fusion
  261.1 38.4 %while.88 = (s32[]{:T(128)}, bf16[2,512,4,128]{3,2,1,0:T(4,128)(2,1)}, bf16[2,4,512,512]{3,2,1,0:T(8,128)(2,1)}, bf16[2,4,512,512]{3,2,1,0:T(8,128)(2,1)}, bf16[...) while((s32[]{:T(128)}, ...), condition=%wide.region_13.14_spmd, body=%wide.region_12.13_spmd.sunk | while | flops 883949568 | bytes 30411028 | solution.py:200
  261.1 1.6 constant_dynamic-slice_fusion.7
  264.3 2.9 bitcast_dynamic-update-slice_fusion.8
  268.5 2.6 convolution_bitcast_fusion.6
  272.1 2.2 fusion.140
  276.7 3.6 bitcast_dynamic-update-slice_fusion.9
  280.3 1.6 constant_dynamic-slice_fusion.7
  283.5 2.9 bitcast_dynamic-update-slice_fusion.8
  287.7 2.6 convolution_bitcast_fusion.6
  291.4 2.2 fusion.140
  295.9 3.6 bitcast_dynamic-update-slice_fusion.9
  299.5 10.2 %fusion.86 = bf16[4096,512]{0,1:T(8,128)(2,1)} fusion(bf16[1024,4096]{1,0:T(8,128)(2,1)} %all-gather.8.cloned.1.call-done, bf16[128,8,4,128]{3,2,1,0:T(4,128)(2,1)} %bitcast.351), kind=kOutput, calls=%fused_computation.122 | convolution fusion | flops 4297064448 | bytes 13631488 | tf_op jit(solution)/shard_map/dot_general | solution.py:204
  313.5 39.7 %while.89 = (s32[]{:T(128)}, bf16[2,512,4,128]{3,2,1,0:T(4,128)(2,1)}, bf16[2,512,4,128]{3,2,1,0:T(4,128)(2,1)}, bf16[2,512,4,128]{3,2,1,0:T(4,128)(2,1)}, bf16[...) while((s32[]{:T(128)}, ...), condition=%wide.region_15.16_spmd, body=%wide.region_14.15_spmd.sunk | while | flops 1008996352 | bytes 24100036 | solution.py:238
  315.6 2.2 fusion.153
  317.8 1.5 fusion.155
  320.4 2.4 fusion.156
  322.9 2.0 fusion.157
  326.3 2.4 constant_dynamic-update-slice_fusion.8
  328.7 2.1 fusion.158
  335.5 2.2 fusion.153
  337.7 1.4 fusion.155
  340.2 2.4 fusion.156
  342.7 2.0 fusion.157
  346.1 2.4 constant_dynamic-update-slice_fusion.8
  348.5 2.1 fusion.158
  353.2 2.5 copy.128
  355.6 2.4 copy.129
  359.2 18.3 %reduce-scatter.2.cloned.1.call-done = bf16[256,512]{0,1:T(8,128)(2,1)} async-done(((bf16[4096,512]{0,1:T(8,128)(2,1)}), bf16[256,512]{0,1:T(8,128)(2,1)}) %reduce-scatter.2.cloned.1.call-update) | async-done | bytes 262160 | tf_op jit(solution)/shard_map/reduce_scatter | solution.py:203
  377.5 1.9 copy.90
  (189 shorter events, 73.7 us)
Async XLA Ops:
  7.2 66.2 %all-gather.10.cloned.1.call-start = ((), (), s32[]{:S(2)}) async-start(), calls=%async_computation.2 | async-start | bytes 4456448 | tf_op jit(solution)/shard_map/all_gather | solution.py:118
  7.9 162.9 %all-gather.8.cloned.1.call-start = ((), (), s32[]{:S(2)}) async-start(), calls=%async_computation.1 | async-start | bytes 9437184 | tf_op jit(solution)/shard_map/all_gather | solution.py:114
  8.6 196.5 %all-gather.12.cloned.1.call-start = ((), (), s32[]{:S(2)}) async-start(), calls=%async_computation.4 | async-start | bytes 2228224 | tf_op jit(solution)/shard_map/all_gather | solution.py:13
  16.3 1.0 copy-start.3
  27.8 8.0 %copy-start.10 = (u32[128]{0:T(128)S(1)}, u32[128]{0:T(128)}, u32[]{:S(2)}) copy-start(u32[128]{0:T(128)} %constant.190) | copy-start | bytes 1540
  32.2 148.6 %copy-start.2 = (bf16[2,512,4,128]{3,1,2,0:T(8,128)(2,1)}, bf16[2,512,4,128]{3,1,2,0:T(8,128)(2,1)S(1)}, u32[]{:S(2)}) copy-start(bf16[2,512,4,128]{3,1,2,0:T(8,128)(2,1)S(1)} %get-tuple-element.1360) | copy-start | bytes 3145732
  33.0 207.8 %all-gather.14.cloned.1.call-start = ((), (), s32[]{:S(2)}) async-start(), calls=%async_computation.5 | async-start | bytes 2228224 | tf_op jit(solution)/shard_map/all_gather | solution.py:13
  192.4 67.5 %copy-start = (f32[2,4,512]{1,2,0:T(8,128)}, f32[2,4,512]{1,2,0:T(8,128)S(1)}, u32[]{:S(2)}) copy-start(f32[2,4,512]{1,2,0:T(8,128)S(1)} %get-tuple-element.1359) | copy-start | bytes 49156
  193.1 64.6 %copy-start.8 = (f32[2,4,128,128]{3,2,1,0:T(8,128)S(1)}, f32[2,4,128,128]{3,2,1,0:T(8,128)}, u32[]{:S(2)}) copy-start(f32[2,4,128,128]{3,2,1,0:T(8,128)} %get-tuple-element.530) | copy-start | bytes 1572868
  193.1 184.4 %reduce-scatter.2.cloned.1.call-start = ((), (), s32[]{:S(2)}) async-start(), calls=%async_computation.3 | async-start | bytes 4456448 | tf_op jit(solution)/shard_map/reduce_scatter | solution.py:203
  262.7 1.6 copy-start.1
  264.1 3.0 copy-start.9
  264.2 3.0 copy-start.5
  264.2 2.9 copy-start.4
  272.1 4.6 %copy-start.6 = (pred[512,512]{1,0:T(8,128)(4,1)S(1)}, pred[512,512]{1,0:T(8,128)(4,1)}, u32[]{:S(2)}) copy-start(pred[512,512]{1,0:T(8,128)(4,1)} %copy-done.5) | copy-start | bytes 786436 | tf_op jit(solution)/shard_map/while
  281.9 1.6 copy-start.1
  283.3 3.0 copy-start.9
  283.4 3.0 copy-start.5
  283.4 2.9 copy-start.4
  291.3 4.6 %copy-start.6 = (pred[512,512]{1,0:T(8,128)(4,1)S(1)}, pred[512,512]{1,0:T(8,128)(4,1)}, u32[]{:S(2)}) copy-start(pred[512,512]{1,0:T(8,128)(4,1)} %copy-done.5) | copy-start | bytes 786436 | tf_op jit(solution)/shard_map/while
  353.2 4.9 %copy-start.7 = (bf16[2,512,4,128]{3,2,1,0:T(4,128)(2,1)S(1)}, bf16[2,512,4,128]{3,2,1,0:T(4,128)(2,1)}, u32[]{:S(2)}) copy-start(bf16[2,512,4,128]{3,2,1,0:T(4,128)(2,1)} %get-tuple-element.532) | copy-start | bytes 3145732
Sparse Core Ops, SparseCore 0:
  9.7 39.5 all-gather.9
  51.5 119.2 all-gather.7
  172.5 32.5 all-gather.11
  206.7 33.9 all-gather.13
  309.9 67.6 reduce-scatter.1
where the time goes:
time: 389 us; the launch traced here: 386 us
  waiting for transfers between devices  136 us (35%)
  matrix products  69.1 us (18%)
  other arithmetic  67.4 us (17%)
  local copies, waits for them, and re-layouts  66.2 us (17%)
  blocking collectives  31.3 us (8%)
  between operations  14.6 us (4%)
    all_gather x1, waiting for transfers between devices, per_device(): full_grad = lax.all_gather(grad_out, 'head', axis=1, tiled=True)  97.4 us
    select_n x32, other arithmetic, turn(): return jax.tree.map(lambda a, b: jnp.where(reached, a, b), new, before)  44.7 us
    unnamed x1, blocking collectives  31.3 us
    all_gather x2, waiting for transfers between devices, prefix(): lax.all_gather(part.astype(kind), axis)  18.9 us
    reduce_scatter x1, waiting for transfers between devices, per_device(): lax.psum_scatter(lax.dot_general(columns, mixed_rows, (((0,), (0,)), ((),...  18.3 us
    dynamic_update_slice x14, local copies, waits for them, and re-layouts, per_device(): mixed, weight_blocks, backed_blocks = lax.map(forward_output, sections[:7])  16.9 us
    dot_general x1, matrix products, per_device(): lax.dot_general(columns, mixed_rows, (((0,), (0,)), ((), ())), preferred_...  10.2 us
    dot_general x1, matrix products, per_device(): jnp.dot(columns, lax.all_gather(out_weight, 'tm', axis=0, tiled=True), pr...  10 us
  transfers between devices with their start and end apart: 5, of which 4 were waited for; matrix products, arithmetic and copies ran while one was open for 34% of the time, Pallas kernels for 0%

commit v1 on v0

--- a/solution.py
+++ b/solution.py
@@ -111,7 +111,9 @@
     tok_rows = query_vectors.shape[0]
     head_count = periods.shape[0]
     block_count = tok_rows // BLK
-    full_grad = lax.all_gather(grad_out, "head", axis=1, tiled=True)
+    full_grad = jnp.concatenate(
+        lax.all_to_all(jnp.stack([grad_out] * lax.axis_size("head")), "head", 0, 0), axis=1
+    )
     columns = full_grad
     grad_mixed = jnp.dot(
         columns,

time: 389 us -> 352 us (0.905)
  waiting for transfers between devices: 136 us -> 89 us
  starting transfers between devices: 0.2 us -> 8.34 us
  local copies, waits for them, and re-layouts: 66.2 us -> 71 us
    all_gather x1 -> x0, waiting for transfers between devices: 97.4 us -> none  [per_device(): full_grad = lax.all_gather(grad_out, 'head', axis=1, tiled=True)]
    all_to_all x0 -> x1, waiting for transfers between devices: none -> 63.7 us  [per_device(): lax.all_to_all(jnp.stack([grad_out] * lax.axis_size('head')), 'head', 0, 0)]
    all_gather x2, waiting for transfers between devices: 18.9 us -> 6.29 us  [prefix(): lax.all_gather(part.astype(kind), axis)]
    all_to_all x0 -> x1, starting transfers between devices: none -> 8.22 us  [per_device(): lax.all_to_all(jnp.stack([grad_out] * lax.axis_size('head')), 'head', 0, 0)]
    another operation x7 -> x8, local copies, waits for them, and re-layouts: 6.87 us -> 11.2 us
    unnamed x20 -> x27, local copies, waits for them, and re-layouts: 9.71 us -> 11.2 us
  transfers between devices with their start and end apart: 5 -> 5, of which waited for: 4 -> 3; matrix products, arithmetic and copies ran while one was open for 34% -> 39% of each run, Pallas kernels for 0% -> 0%
where the time goes in v1:
time: 352 us; the launch traced here: 349 us
  waiting for transfers between devices  89 us (25%)
  local copies, waits for them, and re-layouts  71 us (20%)
  matrix products  69.3 us (20%)
  other arithmetic  65.2 us (19%)
  blocking collectives  30.5 us (9%)
  between operations  14.6 us (4%)
  starting transfers between devices  8.34 us (2%)
    all_to_all x1, waiting for transfers between devices, per_device(): lax.all_to_all(jnp.stack([grad_out] * lax.axis_size('head')), 'head', 0, 0)  63.7 us
    select_n x32, other arithmetic, turn(): return jax.tree.map(lambda a, b: jnp.where(reached, a, b), new, before)  44.6 us
    unnamed x1, blocking collectives  30.5 us
    reduce_scatter x1, waiting for transfers between devices, per_device(): lax.psum_scatter(lax.dot_general(columns, mixed_rows, (((0,), (0,)), ((),...  18.2 us
    dynamic_update_slice x14, local copies, waits for them, and re-layouts, per_device(): mixed, weight_blocks, backed_blocks = lax.map(forward_output, sections[:7])  16.9 us
    unnamed x27, local copies, waits for them, and re-layouts  11.2 us
    dot_general x1, matrix products, per_device(): lax.dot_general(columns, mixed_rows, (((0,), (0,)), ((), ())), preferred_...  10.3 us
    dot_general x1, matrix products, per_device(): jnp.dot(columns, lax.all_gather(out_weight, 'tm', axis=0, tiled=True), pr...  10.2 us
  transfers between devices with their start and end apart: 5, of which 3 were waited for; matrix products, arithmetic and copies ran while one was open for 39% of the time, Pallas kernels for 0%

profile of v1, /device:TPU:6, one launch (start us, length us, event | category | flops | bytes accessed | tf_op | source)
XLA Modules:
  0.0 348.9 jit_solution(15012245707286951665)
XLA Ops:
  7.9 1.5 copy.74
  9.4 4.3 %stack.2 = bf16[8,1024,512]{1,2,0:T(8,128)(2,1)} broadcast(bf16[1024,512]{0,1:T(8,128)(2,1)S(1)} %copy.74), dimensions={1,2} | broadcast | bytes 9437184 | tf_op jit(solution)/shard_map/stack | solution.py:115
  13.7 8.2 %all-to-all-start = ((bf16[8,1024,512]{1,2,0:T(8,128)(2,1)}), bf16[8,1024,512]{1,2,0:T(8,128)(2,1)}, u32[]{:S(2)}, u32[]{:S(2)}) async-start(bf16[8,1024,512]{1,2,0:T(8,128)(2,1)} %stack.2), calls=%async_computation | async-start | bytes 16777216 | tf_op jit(solution)/shard_map/all_to_all | solution.py:115
  22.4 2.4 reduce-window.6
  27.3 2.1 reshape.191
  29.5 1.6 copy.84
  31.1 5.9 %fusion.90 = f32[2,4,512]{1,2,0:T(8,128)} fusion(s32[4]{0:T(128)S(1)} %get-tuple-element.848, s32[2,512]{1,0:T(2,128)S(1)} %add_add_fusion, pred[4]{0:T(512)(128)(4,1)S(1)} %broadcast_compare_fusion), kind=kLoop, calls=%fused_computation.136 | loop fusion | flops 36864 | bytes 20500 | tf_op jit(solution)/shard_map/convert_element_type | solution.py:125
  37.9 4.4 %while.90 = (s32[]{:T(128)}, f32[4,128,128]{2,1,0:T(8,128)S(1)}, f32[2,4,128,128]{3,2,1,0:T(8,128)}, f32[2,4,512]{1,2,0:T(8,128)S(1)}, bf16[2,512,4,128]{1,3,2,0...) while((s32[]{:T(128)}, f32[4,128,128]{2,1,0:T(8,128)S(1)}, ...), condition=%wide.region_5.6_spmd.clone, body=%wide.region_4.5_spmd.clone.sunk | while | flops 68161536 | bytes 2164928 | solution.py:151
  43.9 1.8 copy.79
  47.3 30.5 %all-reduce = bf16[64]{0:T(256)(128)(2,1)S(1)} all-reduce(bf16[64]{0:T(256)(128)(2,1)S(1)} %dynamic-update-slice), channel_id=2, replica_groups=mesh['tm'=16,'head'=8] {'tm'}, use_global_device_ids=true, to_apply=%add | all-reduce | flops 64 | bytes 256
  77.8 2.2 reshape.193
  80.0 2.4 copy.86
  82.5 63.7 %all-to-all-done = bf16[8,1024,512]{1,2,0:T(8,128)(2,1)} async-done(((bf16[8,1024,512]{1,2,0:T(8,128)(2,1)}), bf16[8,1024,512]{1,2,0:T(8,128)(2,1)}, u32[]{:S(2)}, u32[]{:S(2)}) %all-to-all-start) | async-done | bytes 8388640 | tf_op jit(solution)/shard_map/all_to_all | solution.py:115
  146.2 10.2 %convolution_convert_fusion.1 = bf16[1024,512]{1,0:T(8,128)(2,1)} fusion(bf16[1024,4096]{0,1:T(8,128)(2,1)} %bitcast.42, bf16[4096,512]{1,0:T(8,128)(2,1)} %all-gather.7.cloned.1.call-done), kind=kOutput, calls=%fused_computation.123 | convolution fusion | flops 4295491584 | bytes 13631488 | tf_op jit(solution)/shard_map/dot_general | solution.py:118
  156.4 2.2 reshape.198
  160.8 7.2 %while.92 = (s32[]{:T(128)}, f32[4,128,128]{2,1,0:T(8,128)S(1)}, f32[2,4,128,128]{3,2,1,0:T(8,128)}, f32[2,4,512]{1,2,0:T(8,128)S(1)}, bf16[2,512,4,128]{1,3,2,0...) while((s32[]{:T(128)}, f32[4,128,128]{2,1,0:T(8,128)S(1)}, ...), condition=%wide.region_9.10_spmd.clone, body=%wide.region_8.9_spmd.clone.sunk | while | flops 68157440 | bytes 2148499 | solution.py:165
  168.9 28.6 %while.91 = (s32[]{:T(128)}, f32[4,128,128]{2,1,0:T(8,128)}, s32[]{:T(128)}, bf16[16,4]{1,0:T(8,128)(2,1)S(1)}, bf16[16,4,128,128]{3,2,1,0:T(8,128)(2,1)}, /*index=5*/s32[]{:T(128)}, s32[]{:T(128)}) while((s32[]{:T(128)}, f32[4,128,128]{2,1,0:T(8,128)}, s32[]{:T(128)}, bf16[16,4]{1,0:T(8,128)(2,1)S(1)}, ...), condition=%wide.region_7.8_spmd.clone, body=%wide.region_6.7_spmd.clone.sunk | while | flops 327688 | bytes 655505 | solution.py:31
  168.9 1.7 fusion.164
  170.7 1.8 fusion.164
  172.5 1.8 fusion.164
  174.3 1.8 fusion.164
  176.0 1.8 fusion.164
  177.8 1.8 fusion.164
  179.6 1.8 fusion.164
  181.4 1.8 fusion.164
  183.2 1.8 fusion.164
  185.0 1.8 fusion.164
  186.7 1.8 fusion.164
  188.5 1.8 fusion.164
  190.3 1.8 fusion.164
  192.1 1.8 fusion.164
  193.9 1.8 fusion.164
  195.7 1.8 fusion.164
  197.5 6.3 %all-gather.11.cloned.1.call-done = bf16[64,128,128]{2,1,0:T(8,128)(2,1)} async-done(((bf16[4,128,128]{2,1,0:T(8,128)(2,1)}), bf16[64,128,128]{2,1,0:T(8,128)(2,1)}) %all-gather.11.cloned.1.call-update) | async-done | bytes 2097168 | tf_op jit(solution)/shard_map/all_gather | solution.py:13
  203.7 17.0 %while.93 = (s32[]{:T(128)}, f32[4,128,128]{2,1,0:T(8,128)S(1)}, s32[]{:T(128)}, bf16[16,4]{1,0:T(8,128)(2,1)S(1)}, bf16[16,4,128,128]{3,2,1,0:T(8,128)(2,1)}, /*index=5*/s32[]{:T(128)}, s32[]{:T(128)}, s32[]{:T(128)}, s32[]{:T(128)}) while((s32[]{:T(128)}, f32[4,128,128]{2,1,0:T(8,128)S(1)}, s32[]{:T(128)}, ...), condition=%wide.region_11.12_spmd.clone, body=%wide.region_10.11_spmd.clone.sunk | while | flops 327692 | bytes 655567 | solution.py:31
  220.8 2.1 multiply_add_fusion
  224.1 38.4 %while.88 = (s32[]{:T(128)}, bf16[2,512,4,128]{3,2,1,0:T(4,128)(2,1)}, bf16[2,4,512,512]{3,2,1,0:T(8,128)(2,1)}, bf16[2,4,512,512]{3,2,1,0:T(8,128)(2,1)}, bf16[...) while((s32[]{:T(128)}, ...), condition=%wide.region_13.14_spmd, body=%wide.region_12.13_spmd.sunk | while | flops 883949568 | bytes 30411028 | solution.py:202
  224.1 1.6 constant_dynamic-slice_fusion.7
  227.2 2.9 bitcast_dynamic-update-slice_fusion.8
  231.5 2.6 convolution_bitcast_fusion.6
  235.1 2.2 fusion.140
  239.6 3.6 %bitcast_dynamic-update-slice_fusion.9 = bf16[2,4,512,512]{3,2,1,0:T(8,128)(2,1)} fusion(bf16[2,4,512,512]{3,2,1,0:T(8,128)(2,1)} %get-tuple-element.1284, s32[]{:T(128)} %get-tuple-element.1281, f32[4,512]{1,0:T(4,128)} %copy-done.10, f32[4,512]{1,0:T(4,128)S(1)} %get-tuple-element.1121, pred[512,512]{1,0:T(8,128)(4,1)S(1)} %copy-done.6, ...), kind=kOutput, calls=%fused_computation.3.clone.1 | convolution fusion | flops 273678336 | bytes 3433472 | tf_op jit(solution)/shard_map/while/body/eval_jaxpr/thv,shv->hts/dot_general | solution.py:46
  243.3 1.6 constant_dynamic-slice_fusion.7
  246.4 2.9 bitcast_dynamic-update-slice_fusion.8
  250.7 2.6 convolution_bitcast_fusion.6
  254.3 2.2 fusion.140
  258.8 3.7 %bitcast_dynamic-update-slice_fusion.9 = bf16[2,4,512,512]{3,2,1,0:T(8,128)(2,1)} fusion(bf16[2,4,512,512]{3,2,1,0:T(8,128)(2,1)} %get-tuple-element.1284, s32[]{:T(128)} %get-tuple-element.1281, f32[4,512]{1,0:T(4,128)} %copy-done.10, f32[4,512]{1,0:T(4,128)S(1)} %get-tuple-element.1121, pred[512,512]{1,0:T(8,128)(4,1)S(1)} %copy-done.6, ...), kind=kOutput, calls=%fused_computation.3.clone.1 | convolution fusion | flops 273678336 | bytes 3433472 | tf_op jit(solution)/shard_map/while/body/eval_jaxpr/thv,shv->hts/dot_general | solution.py:46
  262.5 10.3 %fusion.86 = bf16[4096,512]{0,1:T(8,128)(2,1)} fusion(bf16[1024,4096]{0,1:T(8,128)(2,1)} %bitcast.42, bf16[128,8,4,128]{3,2,1,0:T(4,128)(2,1)} %bitcast.354), kind=kOutput, calls=%fused_computation.122 | convolution fusion | flops 4297064448 | bytes 13631488 | tf_op jit(solution)/shard_map/dot_general | solution.py:206
  276.6 39.7 %while.89 = (s32[]{:T(128)}, bf16[2,512,4,128]{3,2,1,0:T(4,128)(2,1)}, bf16[2,512,4,128]{3,2,1,0:T(4,128)(2,1)}, bf16[2,512,4,128]{3,2,1,0:T(4,128)(2,1)}, bf16[...) while((s32[]{:T(128)}, ...), condition=%wide.region_15.16_spmd, body=%wide.region_14.15_spmd.sunk | while | flops 1008996352 | bytes 24100036 | solution.py:240
  278.7 2.2 fusion.153
  280.9 1.5 fusion.155
  283.5 2.4 fusion.156
  286.0 2.0 fusion.157
  289.4 2.4 constant_dynamic-update-slice_fusion.8
  291.8 2.1 fusion.158
  298.6 2.2 fusion.153
  303.3 2.4 fusion.156
  305.8 2.0 fusion.157
  309.2 2.4 constant_dynamic-update-slice_fusion.8
  311.6 2.1 fusion.158
  316.3 2.5 copy.130
  318.8 2.4 copy.131
  322.3 18.2 %reduce-scatter.2.cloned.1.call-done = bf16[256,512]{0,1:T(8,128)(2,1)} async-done(((bf16[4096,512]{0,1:T(8,128)(2,1)}), bf16[256,512]{0,1:T(8,128)(2,1)}) %reduce-scatter.2.cloned.1.call-update) | async-done | bytes 262160 | tf_op jit(solution)/shard_map/reduce_scatter | solution.py:205
  340.5 1.9 copy.92
  (196 shorter events, 72.6 us)
Async XLA Ops:
  7.2 139.1 %all-gather.7.cloned.1.call-start = ((), (), s32[]{:S(2)}) async-start(), calls=%async_computation.2 | async-start | bytes 4456448 | tf_op jit(solution)/shard_map/all_gather | solution.py:120
  13.7 8.2 %copy-start.12 = (s32[4]{0:T(128)S(1)}, s32[4]{0:T(128)}, u32[]{:S(2)}) copy-start(s32[4]{0:T(128)} %param.24) | copy-start | bytes 52
  13.7 8.3 %copy-start.11 = (f32[4,1024]{1,0:T(4,128)S(1)}, f32[4,1024]{1,0:T(4,128)}, u32[]{:S(2)}) copy-start(f32[4,1024]{1,0:T(4,128)} %param.25) | copy-start | bytes 49156
  13.7 12.4 %copy-start.9 = (bf16[1024,512]{1,0:T(8,128)(2,1)S(1)}, bf16[1024,512]{1,0:T(8,128)(2,1)}, u32[]{:S(2)}) copy-start(bf16[1024,512]{1,0:T(8,128)(2,1)} %param.21) | copy-start | bytes 3145732
  13.7 132.5 %all-to-all-start = ((bf16[8,1024,512]{1,2,0:T(8,128)(2,1)}), bf16[8,1024,512]{1,2,0:T(8,128)(2,1)}, u32[]{:S(2)}, u32[]{:S(2)}) async-start(bf16[8,1024,512]{1,2,0:T(8,128)(2,1)} %stack.2), calls=%async_computation | async-start | bytes 16777216 | tf_op jit(solution)/shard_map/all_to_all | solution.py:115
  21.9 147.0 %all-gather.9.cloned.1.call-start = ((), (), s32[]{:S(2)}) async-start(), calls=%async_computation.4 | async-start | bytes 2228224 | tf_op jit(solution)/shard_map/all_gather | solution.py:13
  26.4 1.0 copy-start.3
  37.9 7.9 %copy-start.13 = (u32[128]{0:T(128)S(1)}, u32[128]{0:T(128)}, u32[]{:S(2)}) copy-start(u32[128]{0:T(128)} %constant.190) | copy-start | bytes 1540
  42.3 114.1 %copy-start.2 = (bf16[2,512,4,128]{3,1,2,0:T(8,128)(2,1)}, bf16[2,512,4,128]{3,1,2,0:T(8,128)(2,1)S(1)}, u32[]{:S(2)}) copy-start(bf16[2,512,4,128]{3,1,2,0:T(8,128)(2,1)S(1)} %get-tuple-element.1359) | copy-start | bytes 3145732
  43.0 160.7 %all-gather.11.cloned.1.call-start = ((), (), s32[]{:S(2)}) async-start(), calls=%async_computation.5 | async-start | bytes 2228224 | tf_op jit(solution)/shard_map/all_gather | solution.py:13
  168.1 54.8 %copy-start = (f32[2,4,512]{1,2,0:T(8,128)}, f32[2,4,512]{1,2,0:T(8,128)S(1)}, u32[]{:S(2)}) copy-start(f32[2,4,512]{1,2,0:T(8,128)S(1)} %get-tuple-element.1358) | copy-start | bytes 49156
  168.8 52.0 %copy-start.8 = (f32[2,4,128,128]{3,2,1,0:T(8,128)S(1)}, f32[2,4,128,128]{3,2,1,0:T(8,128)}, u32[]{:S(2)}) copy-start(f32[2,4,128,128]{3,2,1,0:T(8,128)} %get-tuple-element.530) | copy-start | bytes 1572868
  168.8 171.7 %reduce-scatter.2.cloned.1.call-start = ((), (), s32[]{:S(2)}) async-start(), calls=%async_computation.3 | async-start | bytes 4456448 | tf_op jit(solution)/shard_map/reduce_scatter | solution.py:205
  225.7 4.4 %copy-start.1 = (bf16[1,512,4,128]{3,2,1,0:T(4,128)(2,1)}, bf16[1,512,4,128]{3,2,1,0:T(4,128)(2,1)S(1)}, u32[]{:S(2)}) copy-start(bf16[1,512,4,128]{3,2,1,0:T(4,128)(2,1)S(1)} %get-tuple-element.1123) | copy-start | bytes 1572868 | tf_op jit(solution)/shard_map/while
  227.1 3.0 copy-start.10
  227.2 2.9 copy-start.5
  227.2 2.9 copy-start.4
  235.1 4.5 %copy-start.6 = (pred[512,512]{1,0:T(8,128)(4,1)S(1)}, pred[512,512]{1,0:T(8,128)(4,1)}, u32[]{:S(2)}) copy-start(pred[512,512]{1,0:T(8,128)(4,1)} %copy-done.5) | copy-start | bytes 786436 | tf_op jit(solution)/shard_map/while
  244.8 4.5 %copy-start.1 = (bf16[1,512,4,128]{3,2,1,0:T(4,128)(2,1)}, bf16[1,512,4,128]{3,2,1,0:T(4,128)(2,1)S(1)}, u32[]{:S(2)}) copy-start(bf16[1,512,4,128]{3,2,1,0:T(4,128)(2,1)S(1)} %get-tuple-element.1123) | copy-start | bytes 1572868 | tf_op jit(solution)/shard_map/while
  246.3 3.0 copy-start.10
  246.4 3.0 copy-start.5
  246.4 3.0 copy-start.4
  254.3 4.5 %copy-start.6 = (pred[512,512]{1,0:T(8,128)(4,1)S(1)}, pred[512,512]{1,0:T(8,128)(4,1)}, u32[]{:S(2)}) copy-start(pred[512,512]{1,0:T(8,128)(4,1)} %copy-done.5) | copy-start | bytes 786436 | tf_op jit(solution)/shard_map/while
  316.3 4.9 %copy-start.7 = (bf16[2,512,4,128]{3,2,1,0:T(4,128)(2,1)S(1)}, bf16[2,512,4,128]{3,2,1,0:T(4,128)(2,1)}, u32[]{:S(2)}) copy-start(bf16[2,512,4,128]{3,2,1,0:T(4,128)(2,1)} %get-tuple-element.532) | copy-start | bytes 3145732
Sparse Core Ops, SparseCore 0:
  9.7 121.9 all-gather.6
  133.3 33.8 all-gather.8
  169.0 34.7 all-gather.10
  272.9 67.5 reduce-scatter.1
